TPU v7x, 256 devices: a whole 4x4x8 slice. The times are simulated.
256 devices in a mesh: section: 16 (over z_lo, y), tensor: 16 (over x, z_hi, core).
Axes of the slice: x: 4, y: 4, z: 8 (z_hi: 2, z_lo: 4; z = z_hi * 4 + z_lo), core: 2. Of those that a mesh axis runs over, the one named last changes fastest.
Arguments:
- inputs_down: bfloat16 [16, 224, 8192], P('section', None, 'tensor'), may hold values from -18 to 18
- inputs_up: bfloat16 [16, 224, 8192], P('section', None, 'tensor'), may hold values from -18 to 18
- grads_down: bfloat16 [16, 224, 8192], P('section', None, 'tensor'), may hold values from -6 to 6
- grads_up: bfloat16 [16, 224, 8192], P('section', None, 'tensor'), may hold values from -6 to 6
- weights_down: bfloat16 [16, 8192, 2048], P('section', 'tensor'), may hold values from -0.5 to 0.5
- weights_up: bfloat16 [16, 8192, 2048], P('section', 'tensor'), may hold values from -0.5 to 0.5
Outputs:
- handed_down: bfloat16 [16, 224, 8192], P('section', None, 'tensor')
- handed_up: bfloat16 [16, 224, 8192], P('section', None, 'tensor')
- returned_down: bfloat16 [16, 224, 8192], P('section', None, 'tensor')
- returned_up: bfloat16 [16, 224, 8192], P('section', None, 'tensor')
- weight_grads: float32 [16, 8192, 2048], P('section', 'tensor')
All inputs are finite; a program needn't handle non-finite values.
Results may differ from a plain program's by a relative error of at most 0.0095.
Values may be sent and summed in bfloat16 or wider, within the bound.
A program may use at most 64 MiB of HBM per device.

v0:
```python
import jax
import jax.numpy as jnp
from jax import lax
from jax.sharding import PartitionSpec as P

D = 8192
HEADS = 64
KV_HEADS = 8
HEAD_DIM = 128


EPS = 1e-05
NEG_BIG = -1e30


def cut_along(x, dim, count):
    before, after = (x.shape[:dim], x.shape[dim + 1 :])
    return jnp.moveaxis(x.reshape(*before, count, -1, *after), dim, 0)


def sum_at_owner(x, axis, dim):
    count = lax.axis_size(axis)
    tiles = lax.all_to_all(cut_along(x, dim, count), axis, 0, 0, tiled=True)
    return jnp.sum(tiles, axis=0)


def shortened(x):

    def short(part):
        return part.astype(jnp.bfloat16) if part.dtype == jnp.float32 else part

    return jax.tree.map(short, x)


def copy_for_each(x, axis):
    count = lax.axis_size(axis)
    return lax.all_to_all(jnp.broadcast_to(x[None], (count, *x.shape)), axis, 0, 0, tiled=True)


def taken_together(x, axis):
    return copy_for_each(x, axis).sum(axis=0)


def passed_along(x, axis, by):
    count = lax.axis_size(axis)
    pairs = [(i, i + by) for i in range(count) if 0 <= i + by < count]
    return lax.ppermute(x, axis, pairs)


def combine_tensor(partial_value):
    share = sum_at_owner(partial_value, "tensor", 1).astype(jnp.bfloat16)
    return lax.all_gather(share, "tensor", axis=1, tiled=True)


def reflect_blocks(parts):
    flipped = tuple((jnp.flip(piece, 1) for piece in parts))
    return jax.tree.map(
        lambda part, own: part.astype(own.dtype),
        lax.all_to_all(shortened(flipped), "section", split_axis=1, concat_axis=1, tiled=True),
        flipped,
    )


def mirror_terms(payload):
    sections = lax.axis_size("section")
    split = tuple(
        (piece.reshape(piece.shape[0], sections, piece.shape[1] // sections) for piece in payload)
    )
    moved = reflect_blocks(
        (
            lax.all_to_all(split[0], "section", split_axis=1, concat_axis=1, tiled=True),
            lax.all_to_all(split[1], "section", split_axis=1, concat_axis=1, tiled=True),
        )
    )
    return tuple(
        (piece.reshape(piece.shape[0], piece.shape[1] * piece.shape[2]) for piece in moved)
    )


def section_pass(inputs, grads, weights):
    tokens, width_here = inputs.shape
    heads_here = width_here // HEAD_DIM
    kv_width = weights.shape[1] // 2
    scale = HEAD_DIM ** (-0.5)
    x_float = inputs.astype(jnp.float32)
    squares = taken_together(jnp.sum(x_float * x_float, axis=1), "tensor")
    scale_rows = lax.rsqrt(squares / D + EPS)[:, None]
    normed = x_float * scale_rows
    hidden = normed.astype(jnp.bfloat16)
    keyval = combine_tensor(jnp.dot(hidden, weights, preferred_element_type=jnp.float32))
    head_ids = lax.axis_index("tensor") * heads_here + jnp.arange(heads_here)
    selector = (head_ids[:, None] // (HEADS // KV_HEADS) == jnp.arange(KV_HEADS)[None, :]).astype(
        jnp.float32
    )
    keys_all = keyval[:, :kv_width].reshape(tokens, KV_HEADS, HEAD_DIM).astype(jnp.float32)
    values_all = keyval[:, kv_width:].reshape(tokens, KV_HEADS, HEAD_DIM).astype(jnp.float32)
    key_rows = jnp.einsum("hj,ljd->lhd", selector, keys_all)
    value_rows = jnp.einsum("hj,ljd->lhd", selector, values_all)
    queries = hidden.reshape(tokens, heads_here, HEAD_DIM).astype(jnp.float32)
    places = jnp.arange(tokens)
    causal = places[:, None] >= places[None, :]
    scores = jnp.einsum("qhd,khd->hqk", queries, key_rows) * scale
    scores = jnp.where(causal[None], scores, NEG_BIG)
    score_peak = jnp.max(scores, axis=-1, keepdims=True)
    score_exp = jnp.exp(scores - score_peak)
    attn_probs = score_exp / jnp.sum(score_exp, axis=-1, keepdims=True)
    probs_low = lax.optimization_barrier(attn_probs.astype(jnp.bfloat16)).astype(jnp.float32)
    attended = jnp.einsum("hqk,khd->qhd", probs_low, value_rows).reshape(tokens, width_here)
    output = (x_float + attended).astype(jnp.bfloat16)
    upstream = grads.astype(jnp.float32).reshape(tokens, heads_here, HEAD_DIM)
    grad_prob = jnp.einsum("qhd,khd->hqk", upstream, value_rows)
    grad_value_heads = jnp.einsum("hqk,qhd->khd", probs_low, upstream)
    grad_score = attn_probs * (grad_prob - jnp.sum(attn_probs * grad_prob, axis=-1, keepdims=True))
    grad_score_low = lax.optimization_barrier(grad_score.astype(jnp.bfloat16)).astype(jnp.float32)
    grad_query = jnp.einsum("hqk,khd->qhd", grad_score_low, key_rows) * scale
    grad_key_heads = jnp.einsum("hqk,qhd->khd", grad_score_low, queries) * scale
    grad_keys = jnp.einsum("hj,lhd->ljd", selector, grad_key_heads).reshape(tokens, kv_width)
    grad_values = jnp.einsum("hj,lhd->ljd", selector, grad_value_heads).reshape(tokens, kv_width)
    grad_kv = combine_tensor(jnp.concatenate([grad_keys, grad_values], axis=1))
    grad_hidden = grad_query.reshape(tokens, width_here) + jnp.dot(
        grad_kv, weights.T, preferred_element_type=jnp.float32
    )
    inner_sum = taken_together(jnp.sum(grad_hidden * normed, axis=1), "tensor")
    grad_input = (
        grads.astype(jnp.float32) + scale_rows * (grad_hidden - normed * (inner_sum / D)[:, None])
    ).astype(jnp.bfloat16)
    grad_weights = jnp.dot(hidden.T, grad_kv, preferred_element_type=jnp.float32)
    return (output, grad_input, grad_weights, hidden, grad_kv)


def on_device(inputs_down, inputs_up, grads_down, grads_up, weights_down, weights_up):
    out_down, back_down, dw_down, hidden_down, gkv_down = section_pass(
        inputs_down[0], grads_down[0], weights_down[0]
    )
    handed_down = passed_along(out_down, "section", 1)
    out_up, back_up, dw_up, hidden_up, gkv_up = section_pass(
        inputs_up[0], grads_up[0], weights_up[0]
    )
    handed_up = passed_along(out_up, "section", -1)
    returned_down = passed_along(back_down, "section", -1)
    returned_up = passed_along(back_up, "section", 1)
    carried_hidden, carried_kv = mirror_terms((hidden_up, gkv_up))
    weight_grads = dw_down + jnp.dot(
        carried_hidden.T, carried_kv, preferred_element_type=jnp.float32
    )
    return (
        handed_down[None],
        handed_up[None],
        returned_down[None],
        returned_up[None],
        weight_grads[None],
    )


def solution(mesh):
    in_specs = (
        P("section", None, "tensor"),
        P("section", None, "tensor"),
        P("section", None, "tensor"),
        P("section", None, "tensor"),
        P("section", "tensor", None),
        P("section", "tensor", None),
    )
    out_specs = (
        P("section", None, "tensor"),
        P("section", None, "tensor"),
        P("section", None, "tensor"),
        P("section", None, "tensor"),
        P("section", "tensor", None),
    )
    return jax.shard_map(
        on_device, mesh=mesh, in_specs=in_specs, out_specs=out_specs, check_vma=False
    )
```

profile of v0, /device:TPU:1, one launch (start us, length us, event | category | flops | bytes accessed | tf_op | source)
XLA Modules:
  0.0 514.8 jit_solution(3485464926994449465)
XLA Ops:
  2.5 12.4 %all-to-all-start.2 = ((f32[16,1,224]{2,1,0:T(1,128)}), f32[16,1,224]{2,1,0:T(1,128)S(1)}, u32[]{:S(2)}, u32[]{:S(2)}) async-start(f32[16,1,224]{2,1,0:T(1,128)} %broadcast_in_dim.40), calls=%async_computation.2 | async-start | bytes 32768 | tf_op jit(solution)/shard_map/all_to_all | solution.py:37
  17.0 7.6 %all-to-all-done.2 = f32[16,1,224]{2,1,0:T(1,128)S(1)} async-done(((f32[16,1,224]{2,1,0:T(1,128)}), f32[16,1,224]{2,1,0:T(1,128)S(1)}, u32[]{:S(2)}, u32[]{:S(2)}) %all-to-all-start.2) | async-done | bytes 14368 | tf_op jit(solution)/shard_map/all_to_all | solution.py:37
  25.2 3.7 all-to-all-start
  29.7 8.9 %all-to-all-done = f32[16,1,224]{2,1,0:T(1,128)S(1)} async-done(((f32[16,1,224]{2,1,0:T(1,128)}), f32[16,1,224]{2,1,0:T(1,128)S(1)}, u32[]{:S(2)}, u32[]{:S(2)}) %all-to-all-start) | async-done | bytes 14368 | tf_op jit(solution)/shard_map/all_to_all | solution.py:37
  38.7 5.7 %all-to-all-start.8 = ((bf16[224,16,32]{0,2,1:T(8,128)(2,1)}), bf16[224,16,32]{0,2,1:T(8,128)(2,1)S(1)}, u32[]{:S(2)}, u32[]{:S(2)}) async-start(bf16[224,16,32]{0,2,1:T(8,128)(2,1)} %multiply_convert_fusion), calls=%async_computation.8 | async-start | bytes 524288 | tf_op jit(solution)/shard_map/all_to_all | solution.py:71
  46.9 3.6 convolution_bitcast_fusion
  50.5 3.7 all-to-all-done.8
  54.2 5.9 %all-to-all-start.3 = ((f32[16,224,128]{2,1,0:T(8,128)}), f32[16,224,128]{2,1,0:T(8,128)}, u32[]{:S(2)}, u32[]{:S(2)}) async-start(f32[16,224,128]{2,1,0:T(8,128)} %convolution_bitcast_fusion), calls=%async_computation.3 | async-start | bytes 3670016 | tf_op jit(solution)/shard_map/all_to_all | solution.py:23
  60.1 4.0 copy.194
  64.1 3.6 convolution_bitcast_fusion.1
  67.8 29.1 %all-to-all-done.3 = f32[16,224,128]{2,1,0:T(8,128)} async-done(((f32[16,224,128]{2,1,0:T(8,128)}), f32[16,224,128]{2,1,0:T(8,128)}, u32[]{:S(2)}, u32[]{:S(2)}) %all-to-all-start.3) | async-done | bytes 1835040 | tf_op jit(solution)/shard_map/all_to_all | solution.py:23
  96.9 6.2 %all-to-all-start.1 = ((f32[16,224,128]{2,1,0:T(8,128)}), f32[16,224,128]{2,1,0:T(8,128)}, u32[]{:S(2)}, u32[]{:S(2)}) async-start(f32[16,224,128]{2,1,0:T(8,128)} %convolution_bitcast_fusion.1), calls=%async_computation.1 | async-start | bytes 3670016 | tf_op jit(solution)/shard_map/all_to_all | solution.py:23
  108.3 66.4 %all_gather.13 = bf16[224,2048]{1,0:T(8,128)(2,1)S(1)} all-gather(bf16[224,128]{1,0:T(8,128)(2,1)S(1)} %reduce_sum.150), channel_id=1, replica_groups=mesh['section'=16,'tensor'=16] {'tensor'}, dimensions={1}, use_global_device_ids=true | all-gather | bytes 974848 | tf_op jit(solution)/shard_map/all_gather | solution.py:52
  184.1 15.2 %all-to-all-start.9 = ((bf16[224,16,32]{0,2,1:T(8,128)(2,1)}), bf16[224,16,32]{0,2,1:T(8,128)(2,1)S(1)}, u32[]{:S(2)}, u32[]{:S(2)}) async-start(bf16[224,16,32]{0,2,1:T(8,128)(2,1)} %rev.8), calls=%async_computation.9 | async-start | bytes 524288 | tf_op jit(solution)/shard_map/all_to_all | solution.py:59
  204.6 4.8 all-to-all-done.9
  209.3 10.3 %all-to-all-start.6 = ((f32[16,224,128]{2,1,0:T(8,128)}), f32[16,224,128]{2,1,0:T(8,128)}, u32[]{:S(2)}, u32[]{:S(2)}) async-start(f32[16,224,128]{2,1,0:T(8,128)} %copy.185), calls=%async_computation.6 | async-start | bytes 3670016 | tf_op jit(solution)/shard_map/all_to_all | solution.py:23
  219.7 70.2 %all_gather.12 = bf16[224,2048]{1,0:T(8,128)(2,1)S(1)} all-gather(bf16[224,128]{1,0:T(8,128)(2,1)S(1)} %reduce_sum.146), channel_id=1, replica_groups=mesh['section'=16,'tensor'=16] {'tensor'}, dimensions={1}, use_global_device_ids=true | all-gather | bytes 974848 | tf_op jit(solution)/shard_map/all_gather | solution.py:52
  300.0 10.4 %all-to-all-start.4 = ((f32[16,224,128]{2,1,0:T(8,128)}), f32[16,224,128]{2,1,0:T(8,128)}, u32[]{:S(2)}, u32[]{:S(2)}) async-start(f32[16,224,128]{2,1,0:T(8,128)} %copy.175), calls=%async_computation.4 | async-start | bytes 3670016 | tf_op jit(solution)/shard_map/all_to_all | solution.py:23
  313.2 69.0 %all_gather.15 = bf16[224,2048]{1,0:T(8,128)(2,1)S(1)} all-gather(bf16[224,128]{1,0:T(8,128)(2,1)S(1)} %reduce_sum.157), channel_id=1, replica_groups=mesh['section'=16,'tensor'=16] {'tensor'}, dimensions={1}, use_global_device_ids=true | all-gather | bytes 974848 | tf_op jit(solution)/shard_map/all_gather | solution.py:52
  385.4 9.6 %all-to-all-start.7 = ((f32[16,1,224]{2,1,0:T(1,128)}), f32[16,1,224]{2,1,0:T(1,128)S(1)}, u32[]{:S(2)}, u32[]{:S(2)}) async-start(f32[16,1,224]{2,1,0:T(1,128)} %broadcast_in_dim.44), calls=%async_computation.7 | async-start | bytes 32768 | tf_op jit(solution)/shard_map/all_to_all | solution.py:37
  396.1 8.6 %all-to-all-done.7 = f32[16,1,224]{2,1,0:T(1,128)S(1)} async-done(((f32[16,1,224]{2,1,0:T(1,128)}), f32[16,1,224]{2,1,0:T(1,128)S(1)}, u32[]{:S(2)}, u32[]{:S(2)}) %all-to-all-start.7) | async-done | bytes 14368 | tf_op jit(solution)/shard_map/all_to_all | solution.py:37
  404.7 5.1 all-to-all-start.10
  413.8 42.8 %all_gather.14 = bf16[224,2048]{1,0:T(8,128)(2,1)S(1)} all-gather(bf16[224,128]{1,0:T(8,128)(2,1)S(1)} %reduce_sum.153), channel_id=1, replica_groups=mesh['section'=16,'tensor'=16] {'tensor'}, dimensions={1}, use_global_device_ids=true | all-gather | bytes 974848 | tf_op jit(solution)/shard_map/all_gather | solution.py:52
  456.7 2.6 fusion.55
  460.0 3.4 all-to-all-start.5
  465.7 7.5 %all-to-all-done.5 = f32[16,1,224]{2,1,0:T(1,128)S(1)} async-done(((f32[16,1,224]{2,1,0:T(1,128)}), f32[16,1,224]{2,1,0:T(1,128)S(1)}, u32[]{:S(2)}, u32[]{:S(2)}) %all-to-all-start.5) | async-done | bytes 14368 | tf_op jit(solution)/shard_map/all_to_all | solution.py:37
  473.1 8.6 %all-to-all-start.11 = ((bf16[224,16,128]{2,0,1:T(8,128)(2,1)}), bf16[224,16,128]{2,0,1:T(8,128)(2,1)S(1)}, u32[]{:S(2)}, u32[]{:S(2)}) async-start(bf16[224,16,128]{2,0,1:T(8,128)(2,1)} %rev.9), calls=%async_computation.11 | async-start | bytes 1835008 | tf_op jit(solution)/shard_map/all_to_all | solution.py:59
  486.5 3.3 collective-permute-start.3
  492.7 4.8 collective-permute-start
  497.5 2.8 fusion.69
  500.3 5.8 %collective-permute-done.2 = bf16[224,512]{1,0:T(8,128)(2,1)S(1)} collective-permute-done((bf16[224,512]{1,0:T(8,128)(2,1)S(1)}, bf16[224,512]{1,0:T(8,128)(2,1)S(1)}, u32[]{:S(2)}, u32[]{:S(2)}) %collective-permute-start.2) | collective-permute-done | bytes 229408 | tf_op jit(solution)/shard_map/ppermute | solution.py:47
  506.2 4.9 add_bitcast_fusion
  (135 shorter events, 63.0 us)
Async XLA Ops:
  0.6 43.7 %copy-start.1 = (bf16[1,512,2048]{2,1,0:T(8,128)(2,1)S(1)}, bf16[1,512,2048]{2,1,0:T(8,128)(2,1)}, u32[]{:S(2)}) copy-start(bf16[1,512,2048]{2,1,0:T(8,128)(2,1)} %param.11) | copy-start | bytes 6291460
  2.5 22.1 %all-to-all-start.2 = ((f32[16,1,224]{2,1,0:T(1,128)}), f32[16,1,224]{2,1,0:T(1,128)S(1)}, u32[]{:S(2)}, u32[]{:S(2)}) async-start(f32[16,1,224]{2,1,0:T(1,128)} %broadcast_in_dim.40), calls=%async_computation.2 | async-start | bytes 32768 | tf_op jit(solution)/shard_map/all_to_all | solution.py:37
  25.2 13.4 %all-to-all-start = ((f32[16,1,224]{2,1,0:T(1,128)}), f32[16,1,224]{2,1,0:T(1,128)S(1)}, u32[]{:S(2)}, u32[]{:S(2)}) async-start(f32[16,1,224]{2,1,0:T(1,128)} %broadcast_in_dim.36), calls=%async_computation | async-start | bytes 32768 | tf_op jit(solution)/shard_map/all_to_all | solution.py:37
  38.7 15.6 %all-to-all-start.8 = ((bf16[224,16,32]{0,2,1:T(8,128)(2,1)}), bf16[224,16,32]{0,2,1:T(8,128)(2,1)S(1)}, u32[]{:S(2)}, u32[]{:S(2)}) async-start(bf16[224,16,32]{0,2,1:T(8,128)(2,1)} %multiply_convert_fusion), calls=%async_computation.8 | async-start | bytes 524288 | tf_op jit(solution)/shard_map/all_to_all | solution.py:71
  54.2 42.6 %all-to-all-start.3 = ((f32[16,224,128]{2,1,0:T(8,128)}), f32[16,224,128]{2,1,0:T(8,128)}, u32[]{:S(2)}, u32[]{:S(2)}) async-start(f32[16,224,128]{2,1,0:T(8,128)} %convolution_bitcast_fusion), calls=%async_computation.3 | async-start | bytes 3670016 | tf_op jit(solution)/shard_map/all_to_all | solution.py:23
  60.1 4.0 copy-start
  67.8 37.2 %copy-start.22 = (bf16[1,224,512]{2,1,0:T(8,128)(2,1)S(1)}, bf16[1,224,512]{2,1,0:T(8,128)(2,1)}, u32[]{:S(2)}) copy-start(bf16[1,224,512]{2,1,0:T(8,128)(2,1)} %param.8) | copy-start | bytes 688132
  96.9 87.2 %all-to-all-start.1 = ((f32[16,224,128]{2,1,0:T(8,128)}), f32[16,224,128]{2,1,0:T(8,128)}, u32[]{:S(2)}, u32[]{:S(2)}) async-start(f32[16,224,128]{2,1,0:T(8,128)} %convolution_bitcast_fusion.1), calls=%async_computation.1 | async-start | bytes 3670016 | tf_op jit(solution)/shard_map/all_to_all | solution.py:23
  176.1 3.9 copy-start.24
  184.1 25.3 %all-to-all-start.9 = ((bf16[224,16,32]{0,2,1:T(8,128)(2,1)}), bf16[224,16,32]{0,2,1:T(8,128)(2,1)S(1)}, u32[]{:S(2)}, u32[]{:S(2)}) async-start(bf16[224,16,32]{0,2,1:T(8,128)(2,1)} %rev.8), calls=%async_computation.9 | async-start | bytes 524288 | tf_op jit(solution)/shard_map/all_to_all | solution.py:59
  209.3 10.3 %copy-start.18 = (bf16[224,16,32]{0,2,1:T(8,128)(2,1)}, bf16[224,16,32]{0,2,1:T(8,128)(2,1)S(1)}, u32[]{:S(2)}) copy-start(bf16[224,16,32]{0,2,1:T(8,128)(2,1)S(1)} %all-to-all-done.9) | copy-start | bytes 688132
  209.3 90.7 %all-to-all-start.6 = ((f32[16,224,128]{2,1,0:T(8,128)}), f32[16,224,128]{2,1,0:T(8,128)}, u32[]{:S(2)}, u32[]{:S(2)}) async-start(f32[16,224,128]{2,1,0:T(8,128)} %copy.185), calls=%async_computation.6 | async-start | bytes 3670016 | tf_op jit(solution)/shard_map/all_to_all | solution.py:23
  290.9 4.3 copy-start.14
  291.3 3.9 copy-start.26
  300.0 10.4 %copy-start.12 = (bf16[4,224,224]{1,2,0:T(8,128)(2,1)S(1)}, bf16[4,224,224]{1,2,0:T(8,128)(2,1)}, u32[]{:S(2)}) copy-start(bf16[4,224,224]{1,2,0:T(8,128)(2,1)} %copy-done.11) | copy-start | bytes 1204228
  300.0 10.4 %copy-start.25 = (bf16[224,4,128]{2,1,0:T(4,128)(2,1)S(1)}, bf16[224,4,128]{2,1,0:T(4,128)(2,1)}, u32[]{:S(2)}) copy-start(bf16[224,4,128]{2,1,0:T(4,128)(2,1)} %copy-done.24) | copy-start | bytes 688132
  300.0 84.8 %all-to-all-start.4 = ((f32[16,224,128]{2,1,0:T(8,128)}), f32[16,224,128]{2,1,0:T(8,128)}, u32[]{:S(2)}, u32[]{:S(2)}) async-start(f32[16,224,128]{2,1,0:T(8,128)} %copy.175), calls=%async_computation.4 | async-start | bytes 3670016 | tf_op jit(solution)/shard_map/all_to_all | solution.py:23
  385.4 19.3 %all-to-all-start.7 = ((f32[16,1,224]{2,1,0:T(1,128)}), f32[16,1,224]{2,1,0:T(1,128)S(1)}, u32[]{:S(2)}, u32[]{:S(2)}) async-start(f32[16,1,224]{2,1,0:T(1,128)} %broadcast_in_dim.44), calls=%async_computation.7 | async-start | bytes 32768 | tf_op jit(solution)/shard_map/all_to_all | solution.py:37
  404.7 54.6 %all-to-all-start.10 = ((bf16[224,16,128]{2,0,1:T(8,128)(2,1)}), bf16[224,16,128]{2,0,1:T(8,128)(2,1)}, u32[]{:S(2)}, u32[]{:S(2)}) async-start(bf16[224,16,128]{2,0,1:T(8,128)(2,1)} %copy_bitcast_fusion), calls=%async_computation.10 | async-start | bytes 1835008 | tf_op jit(solution)/shard_map/all_to_all | solution.py:72
  409.8 46.9 %copy-start.2 = (bf16[1,512,2048]{2,1,0:T(8,128)(2,1)S(1)}, bf16[1,512,2048]{2,1,0:T(8,128)(2,1)}, u32[]{:S(2)}) copy-start(bf16[1,512,2048]{2,1,0:T(8,128)(2,1)} %param.10) | copy-start | bytes 6291460
  459.3 22.4 %copy-start.5 = (bf16[4,224,224]{1,2,0:T(8,128)(2,1)S(1)}, bf16[4,224,224]{1,2,0:T(8,128)(2,1)}, u32[]{:S(2)}) copy-start(bf16[4,224,224]{1,2,0:T(8,128)(2,1)} %copy-done.4) | copy-start | bytes 1204228
  459.3 22.4 %copy-start.9 = (bf16[224,4,128]{2,1,0:T(4,128)(2,1)S(1)}, bf16[224,4,128]{2,1,0:T(4,128)(2,1)}, u32[]{:S(2)}) copy-start(bf16[224,4,128]{2,1,0:T(4,128)(2,1)} %copy-done.8) | copy-start | bytes 688132
  460.0 13.2 %all-to-all-start.5 = ((f32[16,1,224]{2,1,0:T(1,128)}), f32[16,1,224]{2,1,0:T(1,128)S(1)}, u32[]{:S(2)}, u32[]{:S(2)}) async-start(f32[16,1,224]{2,1,0:T(1,128)} %broadcast_in_dim.42), calls=%async_computation.5 | async-start | bytes 32768 | tf_op jit(solution)/shard_map/all_to_all | solution.py:37
  463.4 19.5 %copy-start.7 = (bf16[4,224,224]{1,2,0:T(8,128)(2,1)S(1)}, bf16[4,224,224]{1,2,0:T(8,128)(2,1)}, u32[]{:S(2)}) copy-start(bf16[4,224,224]{1,2,0:T(8,128)(2,1)} %copy-done.6) | copy-start | bytes 1204228
  473.1 33.0 %all-to-all-start.11 = ((bf16[224,16,128]{2,0,1:T(8,128)(2,1)}), bf16[224,16,128]{2,0,1:T(8,128)(2,1)S(1)}, u32[]{:S(2)}, u32[]{:S(2)}) async-start(bf16[224,16,128]{2,0,1:T(8,128)(2,1)} %rev.9), calls=%async_computation.11 | async-start | bytes 1835008 | tf_op jit(solution)/shard_map/all_to_all | solution.py:59
  482.9 8.3 %copy-start.23 = (bf16[1,224,512]{2,1,0:T(8,128)(2,1)S(1)}, bf16[1,224,512]{2,1,0:T(8,128)(2,1)}, u32[]{:S(2)}) copy-start(bf16[1,224,512]{2,1,0:T(8,128)(2,1)} %param.8) | copy-start | bytes 688132
  484.2 7.0 %copy-start.17 = (f32[224,512]{1,0:T(8,128)S(1)}, f32[224,512]{1,0:T(8,128)}, u32[]{:S(2)}) copy-start(f32[224,512]{1,0:T(8,128)} %get-tuple-element.16) | copy-start | bytes 1376260
  486.5 13.8 %collective-permute-start.3 = (bf16[224,512]{1,0:T(8,128)(2,1)}, bf16[224,512]{1,0:T(8,128)(2,1)S(1)}, u32[]{:S(2)}, u32[]{:S(2)}) collective-permute-start(bf16[224,512]{1,0:T(8,128)(2,1)} %get-tuple-element.9), channel_id=1, source_target_pairs={{0,16},{16,32},{32,48},{48,64},{64,80},{80,96},{96,112},{112,128},... | collective-permute-start | bytes 688136 | tf_op jit(solution)/shard_map/ppermute | solution.py:47
  489.8 10.5 %collective-permute-start.1 = (bf16[224,512]{1,0:T(8,128)(2,1)}, bf16[224,512]{1,0:T(8,128)(2,1)}, u32[]{:S(2)}, u32[]{:S(2)}) collective-permute-start(bf16[224,512]{1,0:T(8,128)(2,1)} %get-tuple-element.10), channel_id=1, source_target_pairs={{16,0},{32,16},{48,32},{64,48},{80,64},{96,80},{112,96},{128,112},... | collective-permute-start | bytes 688136 | tf_op jit(solution)/shard_map/ppermute | solution.py:47
  491.4 14.7 %collective-permute-start.2 = (bf16[224,512]{1,0:T(8,128)(2,1)S(1)}, bf16[224,512]{1,0:T(8,128)(2,1)S(1)}, u32[]{:S(2)}, u32[]{:S(2)}) collective-permute-start(bf16[224,512]{1,0:T(8,128)(2,1)S(1)} %get-tuple-element.11), channel_id=1, source_target_pairs={{16,0},{32,16},{48,32},{64,48},{80,64},{96,80},{112,96},{128,112},... | collective-permute-start | bytes 688136 | tf_op jit(solution)/shard_map/ppermute | solution.py:47
  492.7 13.5 %copy-start.19 = (bf16[224,16,32]{0,2,1:T(8,128)(2,1)S(1)}, bf16[224,16,32]{0,2,1:T(8,128)(2,1)}, u32[]{:S(2)}) copy-start(bf16[224,16,32]{0,2,1:T(8,128)(2,1)} %copy-done.18) | copy-start | bytes 688132
  492.7 13.4 %collective-permute-start = (bf16[224,512]{1,0:T(8,128)(2,1)S(1)}, bf16[224,512]{1,0:T(8,128)(2,1)S(1)}, u32[]{:S(2)}, u32[]{:S(2)}) collective-permute-start(bf16[224,512]{1,0:T(8,128)(2,1)S(1)} %get-tuple-element.12), channel_id=1, source_target_pairs={{0,16},{16,32},{32,48},{48,64},{64,80},{80,96},{96,112},{112,128},... | collective-permute-start | bytes 688136 | tf_op jit(solution)/shard_map/ppermute | solution.py:47
  (11 other events, 17.0 us)
where the time goes:
time: 524 us; the launch traced here: 515 us
  blocking collectives  248 us (47%)
  starting transfers between devices  107 us (20%)
  waiting for transfers between devices  76.1 us (15%)
  matrix products  39 us (7%)
  local copies, waits for them, and re-layouts  27.4 us (5%)
  other arithmetic  15.6 us (3%)
    all_gather x4, blocking collectives, combine_tensor(): return lax.all_gather(share, 'tensor', axis=1, tiled=True)  248 us
    all_to_all x4, starting transfers between devices, sum_at_owner(): tiles = lax.all_to_all(cut_along(x, dim, count), axis, 0, 0, tiled=True)  32.8 us
    all_to_all x4, waiting for transfers between devices, copy_for_each(): lax.all_to_all(jnp.broadcast_to(x[None], (count, *x.shape)), axis, 0, 0,...  32.6 us
    all_to_all x4, starting transfers between devices, copy_for_each(): lax.all_to_all(jnp.broadcast_to(x[None], (count, *x.shape)), axis, 0, 0,...  29.1 us
    all_to_all x4, waiting for transfers between devices, sum_at_owner(): tiles = lax.all_to_all(cut_along(x, dim, count), axis, 0, 0, tiled=True)  29.1 us
    all_to_all x2, starting transfers between devices, reflect_blocks(): lax.all_to_all(shortened(flipped), 'section', split_axis=1, concat_axis=1...  23.8 us
    ppermute x4, starting transfers between devices, passed_along(): return lax.ppermute(x, axis, pairs)  10.6 us
  transfers between devices with their start and end apart: 16, of which 8 were waited for; matrix products, arithmetic and copies ran while one was open for 13% of the time, Pallas kernels for 0%

commit v1 on v0

v1 whole, which is shorter than its diff:
```python
import jax
import jax.numpy as jnp
from jax import lax
from jax.experimental import pallas as pl
from jax.experimental.pallas import tpu as pltpu
from jax.sharding import PartitionSpec as P

MESH = pl.DeviceIdType.MESH
F32 = jnp.float32
BF16 = jnp.bfloat16

D = 8192
HEAD_DIM = 128
EPS = 1e-05
NEG_BIG = -1e30
SCALE = HEAD_DIM ** (-0.5)

T = 224
W = 512
HALF = 1024
QH = W // HEAD_DIM
LANES = 256

UP, DOWN, MIRROR = 0, 1, 2


def dot(a, b, ca, cb):
    return lax.dot_general(a, b, (((ca,), (cb,)), ((), ())), preferred_element_type=F32)


def row_of(total):
    return jnp.sum(jnp.transpose(total), axis=0, keepdims=True)


def column_of(row):
    return jnp.transpose(jnp.broadcast_to(row, (128, T)))


def exchange_kernel(sections, *refs):
    (xd_h, xu_h, gd_h, gu_h, wd_h, wu_h) = refs[:6]
    (hd_o, hu_o, rd_o, ru_o, hidt_o, gath_o) = refs[6:12]
    (x, g, w, xm, bias, zeros, hidt) = refs[12:19]
    (psend, precv, xsend, xrecv, acc, zsend, zrecv, kvf, kv, rcol) = refs[19:29]
    (dq, dkv, dkvr, gath, out, gin) = refs[29:35]
    (s0, s1, s2, s3, srp, srx, srz, srm) = refs[35:43]
    (i0, i1, i2, irz, irx, irp) = refs[43:49]
    (lsem, ssem, rsem) = refs[49:52]

    sec = lax.axis_index("section")
    t = lax.axis_index("tensor")
    xi, zi, c = t // 4, (t // 2) % 2, t % 2
    mine, other = c * HALF, (1 - c) * HALF
    head = xi * 2 + zi

    def at(x_, z_, c_):
        return (sec, x_ * 4 + z_ * 2 + c_)

    partner = at(xi, zi, 1 - c)
    zpeer = at(xi, 1 - zi, c)
    xpeer = {d: at((xi + d) % 4, zi, c) for d in (1, 2, 3)}
    mirror = (sections - 1 - sec, t)
    after = (lax.rem(sec + 1, sections), t)
    before = (lax.rem(sec + sections - 1, sections), t)
    has_after = sec < sections - 1
    has_before = sec > 0

    used = [0, 0]

    def remote(src, dst, dev):
        n = used[0]
        used[0] += 1
        return pltpu.make_async_remote_copy(
            src_ref=src, dst_ref=dst, send_sem=ssem.at[n], recv_sem=rsem.at[n],
            device_id=dev, device_id_type=MESH)

    def local(src, dst):
        n = used[1]
        used[1] += 1
        return pltpu.make_async_copy(src, dst, lsem.at[n])

    sends = []

    def go(src, dst, dev):
        copy = remote(src, dst, dev)
        copy.start()
        sends.append(copy)
        return copy

    barrier = pltpu.get_barrier_semaphore()
    for dev in (partner, zpeer, xpeer[1], xpeer[2], xpeer[3], mirror):
        pl.semaphore_signal(barrier, inc=1, device_id=dev, device_id_type=MESH)

    @pl.when(has_after)
    def _():
        pl.semaphore_signal(barrier, inc=1, device_id=after, device_id_type=MESH)

    @pl.when(has_before)
    def _():
        pl.semaphore_signal(barrier, inc=1, device_id=before, device_id_type=MESH)

    load_x = [local(xu_h, x.at[UP]), local(xd_h, x.at[DOWN])]
    load_g = [local(gu_h, g.at[UP]), local(gd_h, g.at[DOWN])]
    mcols, ocols = pl.ds(pl.multiple_of(mine, HALF), HALF), pl.ds(pl.multiple_of(other, HALF), HALF)
    wh = (wu_h, wd_h)
    load_wo = [local(wh[k].at[:, ocols], w.at[k, :, ocols]) for k in (UP, DOWN)]
    load_wm = [local(wh[k].at[:, mcols], w.at[k, :, mcols]) for k in (UP, DOWN)]
    load_x[UP].start()
    load_wo[UP].start()
    load_wm[UP].start()
    load_x[DOWN].start()
    load_wo[DOWN].start()
    load_wm[DOWN].start()
    load_g[UP].start()
    load_g[DOWN].start()

    def block(k, base, d):
        col = pl.multiple_of(base + ((xi + d) % 4) * 256, 128)
        return dot(x[k], w[k, :, pl.ds(col, 256)], 1, 0)

    def squares(k):
        v = x[k].astype(F32)
        v = v * v
        total = v[:, 0:128] + v[:, 128:256] + v[:, 256:384] + v[:, 384:512]
        s0[k : k + 1, 0:T] = row_of(total)

    ORDER = (2, 1, 3, 0)

    def for_partner(k, started):
        load_wo[k].wait()
        copies = {}
        for d in ORDER:
            v = block(k, other, d)
            psend[k, d, 0] = v[:, :128]
            psend[k, d, 1] = v[:, 128:]
            if not started:
                count = 6 + has_after.astype(jnp.int32) + has_before.astype(jnp.int32)
                pl.semaphore_wait(barrier, count)
                started = True
            copies[d] = go(psend.at[k, d], precv.at[k, d], partner)
        return copies

    def for_row(k, from_partner):
        load_wm[k].wait()
        copies = {}
        for d in ORDER:
            v = block(k, mine, d)
            from_partner[d].wait_recv()
            a = v[:, :128] + precv[k, d, 0]
            b = v[:, 128:] + precv[k, d, 1]
            if d == 0:
                acc[k, 0] = a
                acc[k, 1] = b
            else:
                xsend[k, d, 0] = a.astype(BF16)
                xsend[k, d, 1] = b.astype(BF16)
                copies[d] = go(xsend.at[k, d], xrecv.at[k, d], xpeer[d])
        return copies

    zeros[...] = jnp.zeros_like(zeros)
    s0[...] = jnp.zeros_like(s0)
    load_x[UP].wait()
    squares(UP)
    pair_up = for_partner(UP, False)
    mx = go(x.at[UP], xm, mirror)
    load_x[DOWN].wait()
    squares(DOWN)
    sq_pair = go(s0, srp, partner)
    row_up = for_row(UP, pair_up)
    pair_down = for_partner(DOWN, True)
    sq_pair.wait_recv()
    s1[...] = s0[...] + srp[...]
    sq_x = {d: go(s1, srx.at[d], xpeer[d]) for d in (1, 2, 3)}
    row_down = for_row(DOWN, pair_down)

    kk = lax.broadcasted_iota(jnp.int32, (T, QH * T), 0)
    qq = lax.broadcasted_iota(jnp.int32, (T, QH * T), 1)
    for h in range(QH - 1):
        qq = jnp.where(qq >= T, qq - T, qq)
    bias[...] = jnp.where(kk <= qq, 0.0, NEG_BIG)

    for d in (1, 2, 3):
        sq_x[d].wait_recv()
    s2[...] = s1[...] + srx[1] + srx[2] + srx[3]
    sq_z = go(s2, srz, zpeer)

    def for_z(k, row):
        for d in (1, 3, 2):
            row[d].wait_recv()
            acc[k, 0] = acc[k, 0] + xrecv[k, d, 0].astype(F32)
            acc[k, 1] = acc[k, 1] + xrecv[k, d, 1].astype(F32)
        zsend[k] = acc[k, 1 - zi].astype(BF16)
        return go(zsend.at[k], zrecv.at[k], zpeer)

    z_up = for_z(UP, row_up)

    sq_z.wait_recv()
    s3[...] = s2[...] + srz[...]
    sq_m = go(s3, srm, mirror)

    def scale_of(row):
        return column_of(lax.rsqrt(row / D + EPS))

    rcol[UP] = scale_of(s3[0:1, 0:T])
    rcol[DOWN] = scale_of(s3[1:2, 0:T])
    z_down = for_z(DOWN, row_down)

    def final_kv(k, zc):
        zc.wait_recv()
        v = (acc[k, zi] + zrecv[k].astype(F32)) * rcol[k]
        kvf[k] = v
        kv[k, c] = v.astype(BF16)
        return go(kv.at[k, c], kv.at[k, c], partner)

    def attention(k, own):
        load_g[k].wait()
        normed, queries, ups = [], [], []
        for h in range(QH):
            n = x[k, :, h * 128 : h * 128 + 128].astype(F32) * rcol[k]
            queries.append(n.astype(BF16))
            ups.append(g[k, :, h * 128 : h * 128 + 128])
        q = jnp.concatenate(queries, axis=0)
        up = jnp.concatenate(ups, axis=0)
        own.wait_recv()
        key, value = kv[k, 0], kv[k, 1]
        s = dot(key, q, 1, 1) * SCALE + bias[...]
        e = jnp.exp(s - jnp.max(s, axis=0, keepdims=True))
        p = e * (1.0 / jnp.sum(e, axis=0, keepdims=True))
        pl_low = p.astype(BF16)
        dp = dot(value, up, 1, 1)
        ds = p * (dp - jnp.sum(p * dp, axis=0, keepdims=True))
        ds_low = ds.astype(BF16)
        dkv[k, 0] = dot(ds_low, q, 1, 0) * SCALE
        dkv[k, 1] = dot(pl_low, up, 1, 0)
        pair = go(dkv.at[k, 1 - c], dkvr.at[k], partner)
        dqs = dot(ds_low, key, 0, 0) * SCALE
        att = dot(pl_low, value, 0, 0)
        inner = jnp.zeros((T, 128), F32)
        for h in range(QH):
            cols = slice(h * 128, h * 128 + 128)
            rows = slice(h * T, h * T + T)
            xf = x[k, :, cols].astype(F32)
            out[k, :, cols] = (xf + att[rows]).astype(BF16)
            dq[k, h] = dqs[rows]
            inner = inner + dqs[rows] * (xf * rcol[k])
        pair.wait_recv()
        total = dkv[k, c] + dkvr[k]
        low = total.astype(BF16)
        gath[k, c * 8 + head] = low
        i0[k, 0:1, 0:T] = row_of(inner + low.astype(F32) * kvf[k])

    class Gather:
        def __init__(self, k):
            self.k = k
            self.pair = []

        def to(self, b, dev):
            ref = gath.at[self.k, b]
            return go(ref, ref, dev)

        def begin(self):
            b = c * 8 + head
            self.z = self.to(b, zpeer)
            self.x_own = {d: self.to(b, xpeer[d]) for d in (2, 1, 3)}
            self.pair.append(self.to(b, partner))

        def forward_z(self):
            self.z.wait_recv()
            b = c * 8 + xi * 2 + 1 - zi
            self.x_far = {d: self.to(b, xpeer[d]) for d in (2, 1, 3)}
            self.pair.append(self.to(b, partner))

        def forward_x(self, copies, z_):
            for d in (1, 3, 2):
                copies[d].wait_recv()
                b = c * 8 + ((xi + 4 - d) % 4) * 2 + z_
                self.pair.append(self.to(b, partner))

        def finish(self):
            self.forward_x(self.x_own, zi)
            self.forward_x(self.x_far, 1 - zi)

        def arrived(self):
            for copy in self.pair:
                copy.wait_recv()

    def section_send(src, dst, dev, has_to, has_from):
        copy = remote(src, dst, dev)

        @pl.when(has_to)
        def _():
            copy.start()

        return (copy, has_to, has_from)

    crossing = []

    kv_up = final_kv(UP, z_up)
    i0[...] = jnp.zeros_like(i0)
    attention(UP, kv_up)
    up = Gather(UP)
    up.begin()
    inner_z = [go(i0.at[UP], irz.at[UP], zpeer)]
    block_ref = gath.at[UP, c * 8 + head]
    to_mirror = go(block_ref, gath.at[MIRROR, c * 8 + head], mirror)
    crossing.append(section_send(out.at[UP], hu_o, before, has_before, has_after))

    kv_down = final_kv(DOWN, z_down)
    attention(DOWN, kv_down)
    down = Gather(DOWN)
    down.begin()
    inner_z.append(go(i0.at[DOWN], irz.at[DOWN], zpeer))
    crossing.append(section_send(out.at[DOWN], hd_o, after, has_after, has_before))

    def inner_row(k):
        inner_z[k].wait_recv()
        i1[k] = i0[k] + irz[k]
        return {d: go(i1.at[k], irx.at[k, d], xpeer[d]) for d in (1, 2, 3)}

    def inner_pair(k, copies):
        for d in (1, 2, 3):
            copies[d].wait_recv()
        i2[k] = i1[k] + irx[k, 1] + irx[k, 2] + irx[k, 3]
        return go(i2.at[k], irp.at[k], partner)

    up.forward_z()
    ix_up = inner_row(UP)
    to_mirror.wait_recv()
    far = Gather(MIRROR)
    far.begin()
    down.forward_z()
    ix_down = inner_row(DOWN)

    def hidden_rows(v, k, n):
        for h in range(QH):
            cols = slice(h * 128, h * 128 + 128)
            hidt[n, cols, :] = jnp.transpose(v[:, cols].astype(F32) * rcol[k]).astype(BF16)

    hidden_rows(x[DOWN], DOWN, 0)
    sq_m.wait_recv()
    rcol[MIRROR] = scale_of(srm[0:1, 0:T])
    mx.wait_recv()
    hidden_rows(xm[...], MIRROR, 1)
    put_hidt = local(hidt, hidt_o)
    put_hidt.start()

    up.finish()
    ip_up = inner_pair(UP, ix_up)
    far.forward_z()

    def grad_input(k, ip):
        ip.wait_recv()
        mean = column_of((i2[k, 0:1, 0:T] + irp[k, 0:1, 0:T]) * (1.0 / D))
        r = rcol[k]
        for n in range(2):
            rows = slice(n * 256, n * 256 + 256)
            total = jnp.concatenate([dq[k, 2 * n], dq[k, 2 * n + 1]], axis=1)
            for b in range(0, 16, 2):
                pair = jnp.concatenate([gath[k, b], gath[k, b + 1]], axis=1)
                total = total + dot(pair, w[k, rows, b * 128 : b * 128 + 256], 1, 1)
            for m in range(2):
                cols = slice(n * 256 + m * 128, n * 256 + m * 128 + 128)
                gh = total[:, m * 128 : m * 128 + 128]
                normed = x[k, :, cols].astype(F32) * r
                gin[k, :, cols] = (g[k, :, cols].astype(F32) + r * (gh - normed * mean)).astype(BF16)

    up.arrived()
    grad_input(UP, ip_up)
    crossing.append(section_send(gin.at[UP], ru_o, after, has_after, has_before))

    down.finish()
    ip_down = inner_pair(DOWN, ix_down)
    down.arrived()
    grad_input(DOWN, ip_down)
    crossing.append(section_send(gin.at[DOWN], rd_o, before, has_before, has_after))
    put_down = local(gath.at[DOWN], gath_o.at[0])
    put_down.start()

    far.finish()
    far.arrived()
    put_far = local(gath.at[MIRROR], gath_o.at[1])
    put_far.start()

    blank = [local(zeros, ref) for ref in (hu_o, ru_o, hd_o, rd_o)]
    ends = (sec == sections - 1, sec == 0, sec == 0, sec == sections - 1)
    for copy, here in zip(blank, ends):

        @pl.when(here)
        def _(copy=copy):
            copy.start()

    put_hidt.wait()
    put_down.wait()
    put_far.wait()
    for copy, here in zip(blank, ends):

        @pl.when(here)
        def _(copy=copy):
            copy.wait()

    for copy, has_to, has_from in crossing:

        @pl.when(has_to)
        def _(copy=copy):
            copy.wait_send()

        @pl.when(has_from)
        def _(copy=copy):
            copy.wait_recv()

    for copy in sends:
        copy.wait_send()


def exchange(sections, xd, xu, gd, gu, wd, wu):
    act = jax.ShapeDtypeStruct((T, W), BF16)
    hbm = pl.BlockSpec(memory_space=pltpu.HBM)
    free = pl.BlockSpec(memory_space=pl.ANY)
    V = pltpu.VMEM
    small = (8, LANES)
    scratch = [
        V((2, T, W), BF16), V((2, T, W), BF16), V((2, W, 2 * HALF), BF16), V((T, W), BF16),
        V((T, QH * T), F32), V((T, W), BF16), V((2, W, T), BF16),
        V((2, 4, 2, T, 128), F32), V((2, 4, 2, T, 128), F32),
        V((2, 4, 2, T, 128), BF16), V((2, 4, 2, T, 128), BF16),
        V((2, 2, T, 128), F32), V((2, T, 128), BF16), V((2, T, 128), BF16),
        V((2, T, 128), F32), V((2, 2, T, 128), BF16), V((3, T, 128), F32),
        V((2, QH, T, 128), F32), V((2, 2, T, 128), F32), V((2, T, 128), F32),
        V((3, 16, T, 128), BF16), V((2, T, W), BF16), V((2, T, W), BF16),
        V(small, F32), V(small, F32), V(small, F32), V(small, F32),
        V(small, F32), V((4,) + small, F32), V(small, F32), V(small, F32),
        V((2,) + small, F32), V((2,) + small, F32), V((2,) + small, F32),
        V((2,) + small, F32), V((2, 4) + small, F32), V((2,) + small, F32),
        pltpu.SemaphoreType.DMA((16,)), pltpu.SemaphoreType.DMA((104,)), pltpu.SemaphoreType.DMA((104,)),
    ]

    def kernel(*refs):
        exchange_kernel(sections, *refs)

    return pl.pallas_call(
        kernel,
        out_shape=(act, act, act, act, jax.ShapeDtypeStruct((2, W, T), BF16),
                   jax.ShapeDtypeStruct((2, 16, T, 128), BF16)),
        in_specs=[hbm] * 6,
        out_specs=(free,) * 6,
        scratch_shapes=scratch,
        name="exchange",
        compiler_params=pltpu.CompilerParams(
            collective_id=0, has_side_effects=True, vmem_limit_bytes=58 << 20),
    )(xd, xu, gd, gu, wd, wu)


def weights_kernel(hidt, gath, a, b, c, d, dw, ao, bo, co, do):
    for n in range(2):
        total = jnp.zeros((W, 256), F32)
        for m in range(2):
            pair = jnp.concatenate([gath[m, 2 * n], gath[m, 2 * n + 1]], axis=1)
            total = total + dot(hidt[m], pair, 1, 0)
        dw[:, n * 256 : n * 256 + 256] = total
    for src, dst in ((a, ao), (b, bo), (c, co), (d, do)):
        dst[...] = src[...]


def weight_sums(hidt, gath, arrays):
    act = jax.ShapeDtypeStruct((T, W), BF16)
    piece = pl.BlockSpec((T, 128), lambda i: (0, i))
    return pl.pallas_call(
        weights_kernel,
        grid=(4,),
        out_shape=(jax.ShapeDtypeStruct((W, 2 * HALF), F32),) + (act,) * 4,
        in_specs=[pl.BlockSpec((2, W, T), lambda i: (0, 0, 0)),
                  pl.BlockSpec((2, 4, T, 128), lambda i: (0, i, 0, 0))] + [piece] * 4,
        out_specs=(pl.BlockSpec((W, 512), lambda i: (0, i)),) + (piece,) * 4,
        name="weight_sums",
        compiler_params=pltpu.CompilerParams(
            dimension_semantics=("arbitrary",), vmem_limit_bytes=24 << 20),
    )(hidt, gath, *arrays)


def solution(mesh):
    sections = mesh.shape["section"]

    def on_device(xd, xu, gd, gu, wd, wu):
        *arrays, hidt, gath = exchange(sections, xd[0], xu[0], gd[0], gu[0], wd[0], wu[0])
        dw, hd, hu, rd, ru = weight_sums(hidt, gath, arrays)
        return hd[None], hu[None], rd[None], ru[None], dw[None]

    act, wts = P("section", None, "tensor"), P("section", "tensor", None)
    return jax.shard_map(
        on_device, mesh=mesh, in_specs=(act,) * 4 + (wts,) * 2,
        out_specs=(act,) * 4 + (wts,), check_vma=False)
```

time: 524 us -> 69.1 us (0.13); the launches traced: 515 us -> 68.2 us
  blocking collectives: 248 us -> 0 us
  starting transfers between devices: 107 us -> 0 us
  waiting for transfers between devices: 76.1 us -> 0 us
  Pallas kernels: 0 us -> 61.2 us
  matrix products: 39 us -> 0 us
  local copies, waits for them, and re-layouts: 27.4 us -> 6.29 us
  other arithmetic: 15.6 us -> 0 us
    all_gather x4 -> x0, blocking collectives: 248 us -> none  [combine_tensor(): return lax.all_gather(share, 'tensor', axis=1, tiled=True)]
    all_to_all x12 -> x0, starting transfers between devices: 96.5 us -> none  [the longest x4 32.8 us: sum_at_owner(): tiles = lax.all_to_all(cut_along(x, dim, count), axis, 0, 0, tiled=True)]
    all_to_all x12 -> x0, waiting for transfers between devices: 70.2 us -> none  [the longest x4 32.6 us: copy_for_each(): lax.all_to_all(jnp.broadcast_to(x[None], (count, *x.shape)), axis, 0, 0,...]
    pallas_call x0 -> x2, Pallas kernels: none -> 61.2 us  [the longest x1 57.7 us: exchange(): pl.pallas_call(kernel, out_shape=(act, act, act, act, jax.ShapeDtypeStruc...]
    dot_general x24 -> x0, matrix products: 33.9 us -> none  [the longest x2 7.28 us: section_pass(): jnp.dot(hidden, weights, preferred_element_type=jnp.float32)]
    ppermute x4 -> x0, starting transfers between devices: 10.6 us -> none  [passed_along(): return lax.ppermute(x, axis, pairs)]
    reduce_sum x10 -> x0, other arithmetic: 8.79 us -> none  [the longest x4 6.37 us: sum_at_owner(): return jnp.sum(tiles, axis=0)]
    dot_general x2 -> x0, local copies, waits for them, and re-layouts: 6.47 us -> none  [section_pass(): jnp.dot(hidden, weights, preferred_element_type=jnp.float32)]
  transfers between devices with their start and end apart: 16 -> 0, of which waited for: 8 -> 0; matrix products, arithmetic and copies ran while one was open for 13% -> 0% of each run, Pallas kernels for 0% -> 0%
where the time goes in v1:
time: 69.1 us; the launch traced here: 68.2 us
  Pallas kernels  61.2 us (89%)
  local copies, waits for them, and re-layouts  6.29 us (9%)
    pallas_call x1, Pallas kernels, exchange(): pl.pallas_call(kernel, out_shape=(act, act, act, act, jax.ShapeDtypeStruc...  57.7 us
    unnamed x12, local copies, waits for them, and re-layouts  6.29 us
    pallas_call x1, Pallas kernels, weight_sums(): pl.pallas_call(weights_kernel, grid=(4,), out_shape=(jax.ShapeDtypeStruct...  3.55 us

profile of v1, /device:TPU:1, one launch (start us, length us, event | category | flops | bytes accessed | tf_op | source)
XLA Modules:
  0.0 68.2 jit_solution(3715814949951588013)
XLA Ops:
  0.6 57.7 %exchange.1 = (bf16[224,512]{1,0:T(8,128)(2,1)}, bf16[224,512]{1,0:T(8,128)(2,1)}, bf16[224,512]{1,0:T(8,128)(2,1)}, bf16[224,512]{1,0:T(8,128)(2,1)}, bf16[2,51...) custom-call(bf16[224,512]{1,0:T(8,128)(2,1)} %bitcast.13, bf16[224,512]{1,0:T(8,128)(2,1)} %bitcast.14, ...), custom_call_target="tpu_custom_call" | custom-call | tf_op jit(solution)/shard_map/exchange/pallas_call | solution.py:439
  58.3 0.0 copy-start
  58.4 1.5 %copy-done = bf16[2,16,224,128]{3,2,1,0:T(8,128)(2,1)S(1)} copy-done((bf16[2,16,224,128]{3,2,1,0:T(8,128)(2,1)S(1)}, bf16[2,16,224,128]{3,2,1,0:T(8,128)(2,1)}, u32[]{:S(2)}) %copy-start) | copy-done | bytes 1835032
  59.8 0.0 copy-start.1
  59.8 1.0 %copy-done.1 = bf16[2,512,224]{2,1,0:T(8,128)(2,1)S(1)} copy-done((bf16[2,512,224]{2,1,0:T(8,128)(2,1)S(1)}, bf16[2,512,224]{2,1,0:T(8,128)(2,1)}, u32[]{:S(2)}) %copy-start.1) | copy-done | bytes 458776
  60.9 0.0 copy-start.2
  60.9 0.9 %copy-done.2 = bf16[224,512]{1,0:T(8,128)(2,1)S(1)} copy-done((bf16[224,512]{1,0:T(8,128)(2,1)S(1)}, bf16[224,512]{1,0:T(8,128)(2,1)}, u32[]{:S(2)}) %copy-start.2) | copy-done | bytes 229400
  61.8 0.0 copy-start.3
  61.8 0.9 %copy-done.3 = bf16[224,512]{1,0:T(8,128)(2,1)S(1)} copy-done((bf16[224,512]{1,0:T(8,128)(2,1)S(1)}, bf16[224,512]{1,0:T(8,128)(2,1)}, u32[]{:S(2)}) %copy-start.3) | copy-done | bytes 229400
  62.8 0.0 copy-start.4
  62.8 0.9 %copy-done.4 = bf16[224,512]{1,0:T(8,128)(2,1)S(1)} copy-done((bf16[224,512]{1,0:T(8,128)(2,1)S(1)}, bf16[224,512]{1,0:T(8,128)(2,1)}, u32[]{:S(2)}) %copy-start.4) | copy-done | bytes 229400
  63.7 0.0 copy-start.5
  63.7 0.9 %copy-done.5 = bf16[224,512]{1,0:T(8,128)(2,1)S(1)} copy-done((bf16[224,512]{1,0:T(8,128)(2,1)S(1)}, bf16[224,512]{1,0:T(8,128)(2,1)}, u32[]{:S(2)}) %copy-start.5) | copy-done | bytes 229400
  64.6 3.6 %weight_sums.1 = (f32[512,2048]{1,0:T(8,128)}, bf16[224,512]{1,0:T(8,128)(2,1)}, bf16[224,512]{1,0:T(8,128)(2,1)}, bf16[224,512]{1,0:T(8,128)(2,1)}, bf16[224,512]{1,0:T(8,128)(2,1)}) custom-call(bf16[2,512,224]{2,1,0:T(8,128)(2,1)S(1)} %copy-done.1, bf16[2,16,224,128]{3,2,1,0:T(8,128)(2,1)S(1)} %copy-done, bf16[224,512]{1,0:T(8,128)(2,1)S(1)} %copy-done.2, ...), custom_call_target="tpu_custom_call" | custom-call | tf_op jit(solution)/shard_map/weight_sums/pallas_call | solution.py:466
Async XLA Ops:
  58.3 1.5 %copy-start = (bf16[2,16,224,128]{3,2,1,0:T(8,128)(2,1)S(1)}, bf16[2,16,224,128]{3,2,1,0:T(8,128)(2,1)}, u32[]{:S(2)}) copy-start(bf16[2,16,224,128]{3,2,1,0:T(8,128)(2,1)} %get-tuple-element.17.gath) | copy-start | bytes 5505028
  59.8 1.0 %copy-start.1 = (bf16[2,512,224]{2,1,0:T(8,128)(2,1)S(1)}, bf16[2,512,224]{2,1,0:T(8,128)(2,1)}, u32[]{:S(2)}) copy-start(bf16[2,512,224]{2,1,0:T(8,128)(2,1)} %get-tuple-element.16.hidt) | copy-start | bytes 1376260
  60.9 0.9 %copy-start.2 = (bf16[224,512]{1,0:T(8,128)(2,1)S(1)}, bf16[224,512]{1,0:T(8,128)(2,1)}, u32[]{:S(2)}) copy-start(bf16[224,512]{1,0:T(8,128)(2,1)} %get-tuple-element.18.a) | copy-start | bytes 688132
  61.8 0.9 %copy-start.3 = (bf16[224,512]{1,0:T(8,128)(2,1)S(1)}, bf16[224,512]{1,0:T(8,128)(2,1)}, u32[]{:S(2)}) copy-start(bf16[224,512]{1,0:T(8,128)(2,1)} %get-tuple-element.19.b) | copy-start | bytes 688132
  62.8 0.9 %copy-start.4 = (bf16[224,512]{1,0:T(8,128)(2,1)S(1)}, bf16[224,512]{1,0:T(8,128)(2,1)}, u32[]{:S(2)}) copy-start(bf16[224,512]{1,0:T(8,128)(2,1)} %get-tuple-element.20.c) | copy-start | bytes 688132
  63.7 0.9 %copy-start.5 = (bf16[224,512]{1,0:T(8,128)(2,1)S(1)}, bf16[224,512]{1,0:T(8,128)(2,1)}, u32[]{:S(2)}) copy-start(bf16[224,512]{1,0:T(8,128)(2,1)} %get-tuple-element.21.d) | copy-start | bytes 688132

commit v2 on v1

v2 whole, which is shorter than its diff:
```python
import jax
import jax.numpy as jnp
from jax import lax
from jax.experimental import pallas as pl
from jax.experimental.pallas import tpu as pltpu
from jax.sharding import PartitionSpec as P

MESH = pl.DeviceIdType.MESH
F32 = jnp.float32
BF16 = jnp.bfloat16

D = 8192
HEAD_DIM = 128
EPS = 1e-05
NEG_BIG = -1e30
SCALE = HEAD_DIM ** (-0.5)

T = 224
W = 512
HALF = 1024
QH = W // HEAD_DIM
LANES = 256

UP, DOWN, MIRROR = 0, 1, 2


def dot(a, b, ca, cb):
    return lax.dot_general(a, b, (((ca,), (cb,)), ((), ())), preferred_element_type=F32)


def row_of(total):
    return jnp.sum(jnp.transpose(total), axis=0, keepdims=True)


def column_of(row):
    return jnp.transpose(jnp.broadcast_to(row, (128, T)))


def exchange_kernel(sections, *refs):
    (xd_h, xu_h, gd_h, gu_h, wd_h, wu_h) = refs[:6]
    (hd_o, hu_o, rd_o, ru_o, hidt, gath_o) = refs[6:12]
    (x, g, w, xm, bias) = refs[12:17]
    (psend, precv, xsend, xrecv, acc, zsend, zrecv, kvf, kv, rcol) = refs[17:27]
    (dq, dkv, dkvr, gath_up, out, gin) = refs[27:33]
    gh = refs[50]
    (s0, s1, s2, s3, srp, srx, srz, srm) = refs[33:41]
    (i0, i1, i2, irz, irx, irp) = refs[41:47]
    (lsem, ssem, rsem) = refs[47:50]

    gath = (gath_up, gath_o.at[0], gath_o.at[1])

    sec = lax.axis_index("section")
    t = lax.axis_index("tensor")
    xi, zi, c = t // 4, (t // 2) % 2, t % 2
    mine, other = c * HALF, (1 - c) * HALF
    head = xi * 2 + zi

    def at(x_, z_, c_):
        return (sec, x_ * 4 + z_ * 2 + c_)

    partner = at(xi, zi, 1 - c)
    zpeer = at(xi, 1 - zi, c)
    xpeer = {d: at((xi + d) % 4, zi, c) for d in (1, 2, 3)}
    mirror = (sections - 1 - sec, t)
    mirror_z = (sections - 1 - sec, xi * 4 + (1 - zi) * 2 + c)
    after = (lax.rem(sec + 1, sections), t)
    before = (lax.rem(sec + sections - 1, sections), t)
    has_after = sec < sections - 1
    has_before = sec > 0

    used = [0, 0]

    def remote(src, dst, dev):
        n = used[0]
        used[0] += 1
        return pltpu.make_async_remote_copy(
            src_ref=src, dst_ref=dst, send_sem=ssem.at[n], recv_sem=rsem.at[n],
            device_id=dev, device_id_type=MESH)

    def local(src, dst):
        n = used[1]
        used[1] += 1
        return pltpu.make_async_copy(src, dst, lsem.at[n])

    sends = []

    def go(src, dst, dev):
        copy = remote(src, dst, dev)
        copy.start()
        sends.append(copy)
        return copy

    barrier = pltpu.get_barrier_semaphore()
    for dev in (partner, zpeer, xpeer[1], xpeer[2], xpeer[3], mirror, mirror_z):
        pl.semaphore_signal(barrier, inc=1, device_id=dev, device_id_type=MESH)

    @pl.when(has_after)
    def _():
        pl.semaphore_signal(barrier, inc=1, device_id=after, device_id_type=MESH)

    @pl.when(has_before)
    def _():
        pl.semaphore_signal(barrier, inc=1, device_id=before, device_id_type=MESH)

    load_x = [local(xu_h, x.at[UP]), local(xd_h, x.at[DOWN])]
    load_g = [local(gu_h, g.at[UP]), local(gd_h, g.at[DOWN])]
    mcols, ocols = pl.ds(pl.multiple_of(mine, HALF), HALF), pl.ds(pl.multiple_of(other, HALF), HALF)
    wh = (wu_h, wd_h)
    load_wo = [local(wh[k].at[:, ocols], w.at[k, :, ocols]) for k in (UP, DOWN)]
    load_wm = [local(wh[k].at[:, mcols], w.at[k, :, mcols]) for k in (UP, DOWN)]
    load_x[UP].start()
    load_x[DOWN].start()
    load_wo[UP].start()
    load_wm[UP].start()
    load_wo[DOWN].start()
    load_wm[DOWN].start()
    load_g[UP].start()
    load_g[DOWN].start()

    FAR, NEAR = 0, 1
    PAIRS = ((2, 1), (3, 0))

    def block(k, base, side, ds):
        z_ = 1 - zi if side == FAR else zi
        cols = [pl.multiple_of(base + ((xi + d) % 4) * 256 + z_ * 128, 128) for d in ds]
        return dot(x[k], jnp.concatenate([w[k, :, pl.ds(n, 128)] for n in cols], axis=1), 1, 0)

    def squares(k):
        v = x[k].astype(F32)
        v = v * v
        total = v[:, 0:128] + v[:, 128:256] + v[:, 256:384] + v[:, 384:512]
        s0[k : k + 1, 0:T] = row_of(total)

    def for_partner(k, side, first=lambda: None):
        copies = []
        for n, ds in enumerate(PAIRS):
            v = block(k, other, side, ds)
            m = side * 2 + n
            psend[k, m, 0] = v[:, :128]
            psend[k, m, 1] = v[:, 128:]
            if n == 0:
                first()
            copies.append(go(psend.at[k, m], precv.at[k, m], partner))
        return copies

    def for_row(k, side, from_partner, first=lambda: None):
        first()
        for n, ds in enumerate(PAIRS):
            v = block(k, mine, side, ds)
            from_partner[n].wait_recv()
            for i, d in enumerate(ds):
                part = v[:, i * 128 : i * 128 + 128] + precv[k, side * 2 + n, i]
                if d == 0:
                    acc[k, side] = part
                else:
                    xsend[k, side, d] = part.astype(BF16)
        return (2, 1, 3)

    def send_row(k, side, ds):
        return {d: go(xsend.at[k, side, d], xrecv.at[k, side, d], xpeer[d]) for d in ds}

    s0[...] = jnp.zeros_like(s0)
    early = {}

    def after_entry():
        count = 7 + has_after.astype(jnp.int32) + has_before.astype(jnp.int32)
        pl.semaphore_wait(barrier, count)
        early["mx"] = go(x.at[UP], xm, mirror)
        early["sq"] = go(s0, srp, partner)

    def spread_squares():
        early["sq"].wait_recv()
        s1[...] = s0[...] + srp[...]
        early["sq_x"] = {d: go(s1, srx.at[d], xpeer[d]) for d in (1, 2, 3)}

    load_x[UP].wait()
    squares(UP)
    load_x[DOWN].wait()
    squares(DOWN)
    pair, held, row = {}, {}, {}
    load_wo[UP].wait()
    pair[UP, FAR] = for_partner(UP, FAR, after_entry)
    load_wm[UP].wait()
    row[UP, FAR] = send_row(UP, FAR, for_row(UP, FAR, pair[UP, FAR], spread_squares))
    load_wo[DOWN].wait()
    pair[DOWN, FAR] = for_partner(DOWN, FAR)
    pair[UP, NEAR] = for_partner(UP, NEAR)
    load_wm[DOWN].wait()
    held[DOWN, FAR] = for_row(DOWN, FAR, pair[DOWN, FAR])
    row[DOWN, FAR] = send_row(DOWN, FAR, held[DOWN, FAR])
    pair[DOWN, NEAR] = for_partner(DOWN, NEAR)
    held[UP, NEAR] = for_row(UP, NEAR, pair[UP, NEAR])
    sq_x = early["sq_x"]
    for d in (1, 2, 3):
        sq_x[d].wait_recv()
    s2[...] = s1[...] + srx[1] + srx[2] + srx[3]
    sq_z = go(s2, srz, zpeer)
    held[DOWN, NEAR] = for_row(DOWN, NEAR, pair[DOWN, NEAR])

    kk = lax.broadcasted_iota(jnp.int32, (T, QH * T), 0)
    qq = lax.broadcasted_iota(jnp.int32, (T, QH * T), 1)
    for h in range(QH - 1):
        qq = jnp.where(qq >= T, qq - T, qq)
    bias[...] = jnp.where(kk <= qq, 0.0, NEG_BIG)

    def gathered(k, side):
        for d in (1, 3, 2):
            row[k, side][d].wait_recv()
        parts = [xrecv[k, side, d].astype(F32) for d in (1, 3, 2)]
        return acc[k, side] + parts[0] + parts[1] + parts[2]

    def for_z(k):
        zsend[k] = gathered(k, FAR).astype(BF16)
        return go(zsend.at[k], zrecv.at[k], zpeer)

    z_up = for_z(UP)
    row[UP, NEAR] = send_row(UP, NEAR, held[UP, NEAR])
    z_down = for_z(DOWN)
    row[DOWN, NEAR] = send_row(DOWN, NEAR, held[DOWN, NEAR])
    sq_z.wait_recv()
    s3[...] = s2[...] + srz[...]
    sq_m = go(s3, srm, mirror)

    def scale_of(row):
        return column_of(lax.rsqrt(row / D + EPS))

    rcol[UP] = scale_of(s3[0:1, 0:T])
    rcol[DOWN] = scale_of(s3[1:2, 0:T])

    def final_kv(k, zc):
        near = gathered(k, NEAR)
        zc.wait_recv()
        v = (near + zrecv[k].astype(F32)) * rcol[k]
        kvf[k] = v
        kv[k, c] = v.astype(BF16)
        return go(kv.at[k, c], kv.at[k, c], partner)

    def attention(k, own):
        load_g[k].wait()
        normed, queries, ups = [], [], []
        for h in range(QH):
            n = x[k, :, h * 128 : h * 128 + 128].astype(F32) * rcol[k]
            queries.append(n.astype(BF16))
            ups.append(g[k, :, h * 128 : h * 128 + 128])
        q = jnp.concatenate(queries, axis=0)
        up = jnp.concatenate(ups, axis=0)
        own.wait_recv()
        key, value = kv[k, 0], kv[k, 1]
        s = dot(key, q, 1, 1) * SCALE + bias[...]
        e = jnp.exp(s - jnp.max(s, axis=0, keepdims=True))
        p = e * (1.0 / jnp.sum(e, axis=0, keepdims=True))
        pl_low = p.astype(BF16)
        dp = dot(value, up, 1, 1)
        ds = p * (dp - jnp.sum(p * dp, axis=0, keepdims=True))
        ds_low = ds.astype(BF16)
        dkv[k, 0] = dot(ds_low, q, 1, 0) * SCALE
        dkv[k, 1] = dot(pl_low, up, 1, 0)
        pair = go(dkv.at[k, 1 - c], dkvr.at[k], partner)
        dqs = dot(ds_low, key, 0, 0) * SCALE
        att = dot(pl_low, value, 0, 0)
        inner = jnp.zeros((T, 128), F32)
        for h in range(QH):
            cols = slice(h * 128, h * 128 + 128)
            rows = slice(h * T, h * T + T)
            xf = x[k, :, cols].astype(F32)
            out[k, :, cols] = (xf + att[rows]).astype(BF16)
            dq[k, h] = dqs[rows]
            inner = inner + dqs[rows] * (xf * rcol[k])
        pair.wait_recv()
        total = dkv[k, c] + dkvr[k]
        low = total.astype(BF16)
        gath[k][c * 8 + head] = low
        i0[k, 0:1, 0:T] = row_of(inner + low.astype(F32) * kvf[k])

    class Gather:
        def __init__(self, k):
            self.k = k
            self.pair = {0: [], 1: []}

        def to(self, b, dev):
            ref = gath[self.k].at[b]
            return go(ref, ref, dev)

        def begin(self):
            b = c * 8 + head
            if self.k != MIRROR:
                self.z = self.to(b, zpeer)
            self.x_own = {d: self.to(b, xpeer[d]) for d in (2, 1, 3)}
            self.pair[0].append(self.to(b, partner))

        def forward_z(self):
            if self.k != MIRROR:
                self.z.wait_recv()
            b = c * 8 + xi * 2 + 1 - zi
            self.x_far = {d: self.to(b, xpeer[d]) for d in (2, 1, 3)}
            self.pair[1].append(self.to(b, partner))

        def forward_x(self, n):
            copies, z_ = (self.x_far, 1 - zi) if n else (self.x_own, zi)
            for d in (1, 3, 2):
                copies[d].wait_recv()
                b = c * 8 + ((xi + 4 - d) % 4) * 2 + z_
                self.pair[n].append(self.to(b, partner))

        def arrived(self, n):
            for copy in self.pair[n]:
                copy.wait_recv()

    def section_send(src, dst, dev, has_to, has_from):
        copy = remote(src, dst, dev)

        @pl.when(has_to)
        def _():
            copy.start()

        return (copy, has_to, has_from)

    crossing = []

    kv_up = final_kv(UP, z_up)
    i0[...] = jnp.zeros_like(i0)
    attention(UP, kv_up)
    up = Gather(UP)
    up.begin()
    inner_z = [go(i0.at[UP], irz.at[UP], zpeer)]

    kv_down = final_kv(DOWN, z_down)
    attention(DOWN, kv_down)
    down = Gather(DOWN)
    down.begin()
    inner_z.append(go(i0.at[DOWN], irz.at[DOWN], zpeer))

    def inner_row(k):
        inner_z[k].wait_recv()
        i1[k] = i0[k] + irz[k]
        return {d: go(i1.at[k], irx.at[k, d], xpeer[d]) for d in (1, 2, 3)}

    def inner_pair(k, copies):
        for d in (1, 2, 3):
            copies[d].wait_recv()
        i2[k] = i1[k] + irx[k, 1] + irx[k, 2] + irx[k, 3]
        return go(i2.at[k], irp.at[k], partner)

    def part_of(k, n, blocks, total):
        rows = slice(n * 256, n * 256 + 256)
        pair = jnp.concatenate([gath[k][b] for b in blocks], axis=1)
        cols = [pl.multiple_of(b * 128, 128) for b in blocks]
        rhs = jnp.concatenate([w[k, rows, pl.ds(b, 128)] for b in cols], axis=1)
        return total + dot(pair, rhs, 1, 1)

    def grad_near(k):
        for n in range(2):
            total = jnp.concatenate([dq[k, 2 * n], dq[k, 2 * n + 1]], axis=1)
            for i in range(4):
                total = part_of(k, n, [i * 2 + zi, 8 + i * 2 + zi], total)
            gh[k, n] = total

    def grad_input(k, ip, target, dev, has_to, has_from):
        ip.wait_recv()
        mean = column_of((i2[k, 0:1, 0:T] + irp[k, 0:1, 0:T]) * (1.0 / D))
        r = rcol[k]
        for n in range(2):
            total = gh[k, n]
            for i in range(4):
                total = part_of(k, n, [i * 2 + 1 - zi, 9 + i * 2 - zi], total)
            for m in range(2):
                cols = slice(n * 256 + m * 128, n * 256 + m * 128 + 128)
                normed = x[k, :, cols].astype(F32) * r
                value = total[:, m * 128 : m * 128 + 128] - normed * mean
                gin[k, :, cols] = (g[k, :, cols].astype(F32) + r * value).astype(BF16)
            cols = slice(n * 256, n * 256 + 256)
            crossing.append(section_send(gin.at[k, :, cols], target.at[:, cols], dev, has_to, has_from))

    def hidden_rows(v, k, n):
        for h in range(QH):
            cols = slice(h * 128, h * 128 + 128)
            hidt[n, cols, :] = jnp.transpose(v[:, cols].astype(F32) * rcol[k]).astype(BF16)

    hidden_rows(x[DOWN], DOWN, 0)
    sq_m.wait_recv()
    rcol[MIRROR] = scale_of(srm[0:1, 0:T])
    early["mx"].wait_recv()
    hidden_rows(xm[...], MIRROR, 1)
    up.forward_z()
    ix_up = inner_row(UP)
    ref = gath[UP].at[c * 8 + head]
    to_mirror = [go(ref, gath[MIRROR].at[c * 8 + head], dev) for dev in (mirror, mirror_z)]
    up.forward_x(0)
    up.arrived(0)
    grad_near(UP)
    down.forward_x(0)
    down.forward_z()
    ix_down = inner_row(DOWN)
    crossing.append(section_send(out.at[UP], hu_o, before, has_before, has_after))
    crossing.append(section_send(out.at[DOWN], hd_o, after, has_after, has_before))
    down.arrived(0)
    grad_near(DOWN)
    up.forward_x(1)
    ip_up = inner_pair(UP, ix_up)
    up.arrived(1)
    grad_input(UP, ip_up, ru_o, after, has_after, has_before)
    far = Gather(MIRROR)
    to_mirror[0].wait_recv()
    far.begin()
    to_mirror[1].wait_recv()
    far.forward_z()
    down.forward_x(1)
    ip_down = inner_pair(DOWN, ix_down)
    down.arrived(1)
    grad_input(DOWN, ip_down, rd_o, before, has_before, has_after)
    far.forward_x(0)
    far.forward_x(1)
    far.arrived(0)
    far.arrived(1)

    for ref, here in ((hu_o, sec == sections - 1), (ru_o, sec == 0), (hd_o, sec == 0), (rd_o, sec == sections - 1)):

        @pl.when(here)
        def _(ref=ref):
            ref[...] = jnp.zeros_like(ref)

    for copy, has_to, has_from in crossing:

        @pl.when(has_to)
        def _(copy=copy):
            copy.wait_send()

        @pl.when(has_from)
        def _(copy=copy):
            copy.wait_recv()

    for copy in sends:
        copy.wait_send()


def exchange(sections, xd, xu, gd, gu, wd, wu):
    act = pltpu.VMEM((T, W), BF16)
    hbm = pl.BlockSpec(memory_space=pltpu.HBM)
    vmem = pl.BlockSpec(memory_space=pltpu.VMEM)
    V = pltpu.VMEM
    small = (8, LANES)
    scratch = [
        V((2, T, W), BF16), V((2, T, W), BF16), V((2, W, 2 * HALF), BF16), V((T, W), BF16),
        V((T, QH * T), F32),
        V((2, 4, 2, T, 128), F32), V((2, 4, 2, T, 128), F32),
        V((2, 2, 4, T, 128), BF16), V((2, 2, 4, T, 128), BF16),
        V((2, 2, T, 128), F32), V((2, T, 128), BF16), V((2, T, 128), BF16),
        V((2, T, 128), F32), V((2, 2, T, 128), BF16), V((3, T, 128), F32),
        V((2, QH, T, 128), F32), V((2, 2, T, 128), F32), V((2, T, 128), F32),
        V((16, T, 128), BF16), V((2, T, W), BF16), V((2, T, W), BF16),
        V(small, F32), V(small, F32), V(small, F32), V(small, F32),
        V(small, F32), V((4,) + small, F32), V(small, F32), V(small, F32),
        V((2,) + small, F32), V((2,) + small, F32), V((2,) + small, F32),
        V((2,) + small, F32), V((2, 4) + small, F32), V((2,) + small, F32),
        pltpu.SemaphoreType.DMA((8,)), pltpu.SemaphoreType.DMA((104,)), pltpu.SemaphoreType.DMA((104,)),
        V((2, 2, T, 256), F32),
    ]

    def kernel(*refs):
        exchange_kernel(sections, *refs)

    return pl.pallas_call(
        kernel,
        out_shape=(act, act, act, act, pltpu.VMEM((2, W, T), BF16),
                   pltpu.VMEM((2, 16, T, 128), BF16)),
        in_specs=[hbm] * 6,
        out_specs=(vmem,) * 6,
        scratch_shapes=scratch,
        name="exchange",
        compiler_params=pltpu.CompilerParams(
            collective_id=0, has_side_effects=True, vmem_limit_bytes=58 << 20),
    )(xd, xu, gd, gu, wd, wu)


def weights_kernel(hidt, gath, a, b, c, d, dw, ao, bo, co, do):
    for n in range(2):
        total = jnp.zeros((W, 256), F32)
        for m in range(2):
            pair = jnp.concatenate([gath[m, 2 * n], gath[m, 2 * n + 1]], axis=1)
            total = total + dot(hidt[m], pair, 1, 0)
        dw[:, n * 256 : n * 256 + 256] = total
    for src, dst in ((a, ao), (b, bo), (c, co), (d, do)):
        dst[...] = src[...]


def weight_sums(hidt, gath, arrays):
    act = jax.ShapeDtypeStruct((T, W), BF16)
    piece = pl.BlockSpec((T, 128), lambda i: (0, i))
    return pl.pallas_call(
        weights_kernel,
        grid=(4,),
        out_shape=(jax.ShapeDtypeStruct((W, 2 * HALF), F32),) + (act,) * 4,
        in_specs=[pl.BlockSpec((2, W, T), lambda i: (0, 0, 0)),
                  pl.BlockSpec((2, 4, T, 128), lambda i: (0, i, 0, 0))] + [piece] * 4,
        out_specs=(pl.BlockSpec((W, 512), lambda i: (0, i)),) + (piece,) * 4,
        name="weight_sums",
        compiler_params=pltpu.CompilerParams(
            dimension_semantics=("arbitrary",), vmem_limit_bytes=24 << 20),
    )(hidt, gath, *arrays)


def solution(mesh):
    sections = mesh.shape["section"]

    def on_device(xd, xu, gd, gu, wd, wu):
        *arrays, hidt, gath = exchange(sections, xd[0], xu[0], gd[0], gu[0], wd[0], wu[0])
        dw, hd, hu, rd, ru = weight_sums(hidt, gath, arrays)
        return hd[None], hu[None], rd[None], ru[None], dw[None]

    act, wts = P("section", None, "tensor"), P("section", "tensor", None)
    return jax.shard_map(
        on_device, mesh=mesh, in_specs=(act,) * 4 + (wts,) * 2,
        out_specs=(act,) * 4 + (wts,), check_vma=False)
```

time: 69.1 us -> 55 us (0.80); the launches traced: 68.2 us -> 54.9 us
  Pallas kernels: 61.2 us -> 54.3 us
  local copies, waits for them, and re-layouts: 6.29 us -> 0 us
    pallas_call x1, Pallas kernels: 57.7 us -> 50.7 us  [exchange(): pl.pallas_call(kernel, out_shape=(act, act, act, act, pltpu.VMEM((2, W, T...]
    unnamed x12 -> x0, local copies, waits for them, and re-layouts: 6.29 us -> none
where the time goes in v2:
time: 55 us; the launch traced here: 54.9 us
  Pallas kernels  54.3 us (99%)
  between operations  0.64 us (1%)
    pallas_call x1, Pallas kernels, exchange(): pl.pallas_call(kernel, out_shape=(act, act, act, act, pltpu.VMEM((2, W, T...  50.7 us
    pallas_call x1, Pallas kernels, weight_sums(): pl.pallas_call(weights_kernel, grid=(4,), out_shape=(jax.ShapeDtypeStruct...  3.58 us

profile of v2, /device:TPU:1, one launch (start us, length us, event | category | flops | bytes accessed | tf_op | source)
XLA Modules:
  0.0 54.9 jit_solution(17865479108389409449)
XLA Ops:
  0.6 50.7 %exchange.1 = (bf16[224,512]{1,0:T(8,128)(2,1)S(1)}, bf16[224,512]{1,0:T(8,128)(2,1)S(1)}, bf16[224,512]{1,0:T(8,128)(2,1)S(1)}, bf16[224,512]{1,0:T(8,128)(2,1)...) custom-call(bf16[224,512]{1,0:T(8,128)(2,1)} %bitcast.13, bf16[224,512]{1,0:T(8,128)(2,1)} %bitcast.14, ...), custom_call_target="tpu_custom_call" | custom-call | tf_op jit(solution)/shard_map/exchange/pallas_call | solution.py:462
  51.4 3.6 %weight_sums.1 = (f32[512,2048]{1,0:T(8,128)}, bf16[224,512]{1,0:T(8,128)(2,1)}, bf16[224,512]{1,0:T(8,128)(2,1)}, bf16[224,512]{1,0:T(8,128)(2,1)}, bf16[224,512]{1,0:T(8,128)(2,1)}) custom-call(bf16[2,512,224]{2,1,0:T(8,128)(2,1)S(1)} %get-tuple-element.16.hidt, bf16[2,16,224,128]{3,2,1,0:T(8,128)(2,1)S(1)} %get-tuple-element.17.gath, ...), custom_call_target="tpu_custom_call" | custom-call | tf_op jit(solution)/shard_map/weight_sums/pallas_call | solution.py:489

commit v3 on v2

--- a/solution.py
+++ b/solution.py
@@ -22,6 +22,7 @@
 LANES = 256
 
 UP, DOWN, MIRROR = 0, 1, 2
+LOADS, SENDS, COPIES = 8, 58, 95
 
 
 def dot(a, b, ca, cb):
@@ -68,13 +69,17 @@
     has_after = sec < sections - 1
     has_before = sec > 0
 
-    used = [0, 0]
-
-    def remote(src, dst, dev):
+    used = [0, 0, 0]
+    idle = []
+
+    def remote(src, dst, dev, m=None):
         n = used[0]
         used[0] += 1
+        if m is None:
+            m = used[2]
+            used[2] += 1
         return pltpu.make_async_remote_copy(
-            src_ref=src, dst_ref=dst, send_sem=ssem.at[n], recv_sem=rsem.at[n],
+            src_ref=src, dst_ref=dst, send_sem=ssem.at[m], recv_sem=rsem.at[n],
             device_id=dev, device_id_type=MESH)
 
     def local(src, dst):
@@ -85,10 +90,21 @@
     sends = []
 
     def go(src, dst, dev):
-        copy = remote(src, dst, dev)
+        if idle:
+            m = idle.pop()
+        else:
+            m = used[2]
+            used[2] += 1
+        copy = remote(src, dst, dev, m)
         copy.start()
-        sends.append(copy)
+        sends.append((copy, m))
         return copy
+
+    def drain(count):
+        for copy, m in sends[:count]:
+            copy.wait_send()
+            idle.append(m)
+        del sends[:count]
 
     barrier = pltpu.get_barrier_semaphore()
     for dev in (partner, zpeer, xpeer[1], xpeer[2], xpeer[3], mirror, mirror_z):
@@ -320,6 +336,7 @@
     kv_up = final_kv(UP, z_up)
     i0[...] = jnp.zeros_like(i0)
     attention(UP, kv_up)
+    first_part = len(sends)
     up = Gather(UP)
     up.begin()
     inner_z = [go(i0.at[UP], irz.at[UP], zpeer)]
@@ -381,6 +398,7 @@
     rcol[MIRROR] = scale_of(srm[0:1, 0:T])
     early["mx"].wait_recv()
     hidden_rows(xm[...], MIRROR, 1)
+    drain(first_part)
     up.forward_z()
     ix_up = inner_row(UP)
     ref = gath[UP].at[c * 8 + head]
@@ -391,6 +409,7 @@
     down.forward_x(0)
     down.forward_z()
     ix_down = inner_row(DOWN)
+    second_part = len(sends)
     crossing.append(section_send(out.at[UP], hu_o, before, has_before, has_after))
     crossing.append(section_send(out.at[DOWN], hd_o, after, has_after, has_before))
     down.arrived(0)
@@ -398,16 +417,17 @@
     up.forward_x(1)
     ip_up = inner_pair(UP, ix_up)
     up.arrived(1)
-    grad_input(UP, ip_up, ru_o, after, has_after, has_before)
     far = Gather(MIRROR)
     to_mirror[0].wait_recv()
     far.begin()
+    grad_input(UP, ip_up, ru_o, after, has_after, has_before)
     to_mirror[1].wait_recv()
     far.forward_z()
     down.forward_x(1)
     ip_down = inner_pair(DOWN, ix_down)
     down.arrived(1)
     grad_input(DOWN, ip_down, rd_o, before, has_before, has_after)
+    drain(second_part)
     far.forward_x(0)
     far.forward_x(1)
     far.arrived(0)
@@ -429,8 +449,8 @@
         def _(copy=copy):
             copy.wait_recv()
 
-    for copy in sends:
-        copy.wait_send()
+    drain(len(sends))
+    assert used[0] == COPIES and used[1] == LOADS and used[2] == SENDS, used
 
 
 def exchange(sections, xd, xu, gd, gu, wd, wu):
@@ -452,7 +472,7 @@
         V(small, F32), V((4,) + small, F32), V(small, F32), V(small, F32),
         V((2,) + small, F32), V((2,) + small, F32), V((2,) + small, F32),
         V((2,) + small, F32), V((2, 4) + small, F32), V((2,) + small, F32),
-        pltpu.SemaphoreType.DMA((8,)), pltpu.SemaphoreType.DMA((104,)), pltpu.SemaphoreType.DMA((104,)),
+        pltpu.SemaphoreType.DMA((LOADS,)), pltpu.SemaphoreType.DMA((SENDS,)), pltpu.SemaphoreType.DMA((COPIES,)),
         V((2, 2, T, 256), F32),
     ]
 
@@ -472,30 +492,35 @@
     )(xd, xu, gd, gu, wd, wu)
 
 
-def weights_kernel(hidt, gath, a, b, c, d, dw, ao, bo, co, do):
-    for n in range(2):
+def weights_kernel(hidt, gath, a, b, c, d, dw, ao, bo, co, do, stage, sems):
+    copies = [pltpu.make_async_copy(src, dst, sems.at[8 + n])
+              for n, (src, dst) in enumerate(((a, ao), (b, bo), (c, co), (d, do)))]
+    for copy in copies:
+        copy.start()
+    for n in range(8):
         total = jnp.zeros((W, 256), F32)
         for m in range(2):
             pair = jnp.concatenate([gath[m, 2 * n], gath[m, 2 * n + 1]], axis=1)
             total = total + dot(hidt[m], pair, 1, 0)
-        dw[:, n * 256 : n * 256 + 256] = total
-    for src, dst in ((a, ao), (b, bo), (c, co), (d, do)):
-        dst[...] = src[...]
+        stage[n] = total
+        copies.append(pltpu.make_async_copy(stage.at[n], dw.at[:, n * 256 : n * 256 + 256], sems.at[n]))
+        copies[-1].start()
+    for copy in copies:
+        copy.wait()
 
 
 def weight_sums(hidt, gath, arrays):
     act = jax.ShapeDtypeStruct((T, W), BF16)
-    piece = pl.BlockSpec((T, 128), lambda i: (0, i))
+    vmem = pl.BlockSpec(memory_space=pltpu.VMEM)
+    hbm = pl.BlockSpec(memory_space=pltpu.HBM)
     return pl.pallas_call(
         weights_kernel,
-        grid=(4,),
         out_shape=(jax.ShapeDtypeStruct((W, 2 * HALF), F32),) + (act,) * 4,
-        in_specs=[pl.BlockSpec((2, W, T), lambda i: (0, 0, 0)),
-                  pl.BlockSpec((2, 4, T, 128), lambda i: (0, i, 0, 0))] + [piece] * 4,
-        out_specs=(pl.BlockSpec((W, 512), lambda i: (0, i)),) + (piece,) * 4,
+        in_specs=[vmem] * 6,
+        out_specs=(hbm,) * 5,
+        scratch_shapes=[pltpu.VMEM((8, W, 256), F32), pltpu.SemaphoreType.DMA((12,))],
         name="weight_sums",
-        compiler_params=pltpu.CompilerParams(
-            dimension_semantics=("arbitrary",), vmem_limit_bytes=24 << 20),
+        compiler_params=pltpu.CompilerParams(vmem_limit_bytes=24 << 20),
     )(hidt, gath, *arrays)
 
 

time: 55 us -> 53.4 us (0.971)
  Pallas kernels: 54.3 us -> 52.7 us
    pallas_call x1, Pallas kernels: 3.58 us -> 2.54 us  [weight_sums(): pl.pallas_call(weights_kernel, out_shape=(jax.ShapeDtypeStruct((W, 2 * HA...]
    pallas_call x1, Pallas kernels: 50.7 us -> 50.2 us  [exchange(): pl.pallas_call(kernel, out_shape=(act, act, act, act, pltpu.VMEM((2, W, T...]
where the time goes in v3:
time: 53.4 us; the launch traced here: 53.3 us
  Pallas kernels  52.7 us (99%)
  between operations  0.64 us (1%)
    pallas_call x1, Pallas kernels, exchange(): pl.pallas_call(kernel, out_shape=(act, act, act, act, pltpu.VMEM((2, W, T...  50.2 us
    pallas_call x1, Pallas kernels, weight_sums(): pl.pallas_call(weights_kernel, out_shape=(jax.ShapeDtypeStruct((W, 2 * HA...  2.54 us

profile of v3, /device:TPU:1, one launch (start us, length us, event | category | flops | bytes accessed | tf_op | source)
XLA Modules:
  0.0 53.3 jit_solution(5262552985277597760)
XLA Ops:
  0.6 50.2 %exchange.1 = (bf16[224,512]{1,0:T(8,128)(2,1)S(1)}, bf16[224,512]{1,0:T(8,128)(2,1)S(1)}, bf16[224,512]{1,0:T(8,128)(2,1)S(1)}, bf16[224,512]{1,0:T(8,128)(2,1)...) custom-call(bf16[224,512]{1,0:T(8,128)(2,1)} %bitcast.13, bf16[224,512]{1,0:T(8,128)(2,1)} %bitcast.14, ...), custom_call_target="tpu_custom_call" | custom-call | tf_op jit(solution)/shard_map/exchange/pallas_call | solution.py:482
  50.8 2.5 %weight_sums.1 = (f32[512,2048]{1,0:T(8,128)}, bf16[224,512]{1,0:T(8,128)(2,1)}, bf16[224,512]{1,0:T(8,128)(2,1)}, bf16[224,512]{1,0:T(8,128)(2,1)}, bf16[224,512]{1,0:T(8,128)(2,1)}) custom-call(bf16[2,512,224]{2,1,0:T(8,128)(2,1)S(1)} %get-tuple-element.16.hidt, bf16[2,16,224,128]{3,2,1,0:T(8,128)(2,1)S(1)} %get-tuple-element.17.gath, ...), custom_call_target="tpu_custom_call" | custom-call | tf_op jit(solution)/shard_map/weight_sums/pallas_call | solution.py:516

commit v4 on v3

--- a/solution.py
+++ b/solution.py
@@ -401,11 +401,11 @@
     drain(first_part)
     up.forward_z()
     ix_up = inner_row(UP)
-    ref = gath[UP].at[c * 8 + head]
-    to_mirror = [go(ref, gath[MIRROR].at[c * 8 + head], dev) for dev in (mirror, mirror_z)]
     up.forward_x(0)
     up.arrived(0)
     grad_near(UP)
+    ref = gath[UP].at[c * 8 + head]
+    to_mirror = [go(ref, gath[MIRROR].at[c * 8 + head], dev) for dev in (mirror, mirror_z)]
     down.forward_x(0)
     down.forward_z()
     ix_down = inner_row(DOWN)

time: 53.4 us -> 53 us (level)
  no operation moved by 1% of the time
where the time goes in v4:
time: 53 us; the launch traced here: 52.9 us
  Pallas kernels  52.2 us (98%)
  between operations  0.64 us (1%)
    pallas_call x1, Pallas kernels, exchange(): pl.pallas_call(kernel, out_shape=(act, act, act, act, pltpu.VMEM((2, W, T...  49.7 us
    pallas_call x1, Pallas kernels, weight_sums(): pl.pallas_call(weights_kernel, out_shape=(jax.ShapeDtypeStruct((W, 2 * HA...  2.54 us

profile of v4, /device:TPU:1, one launch (start us, length us, event | category | flops | bytes accessed | tf_op | source)
XLA Modules:
  0.0 52.9 jit_solution(16214927449459972664)
XLA Ops:
  0.6 49.7 %exchange.1 = (bf16[224,512]{1,0:T(8,128)(2,1)S(1)}, bf16[224,512]{1,0:T(8,128)(2,1)S(1)}, bf16[224,512]{1,0:T(8,128)(2,1)S(1)}, bf16[224,512]{1,0:T(8,128)(2,1)...) custom-call(bf16[224,512]{1,0:T(8,128)(2,1)} %bitcast.13, bf16[224,512]{1,0:T(8,128)(2,1)} %bitcast.14, ...), custom_call_target="tpu_custom_call" | custom-call | tf_op jit(solution)/shard_map/exchange/pallas_call | solution.py:482
  50.3 2.5 %weight_sums.1 = (f32[512,2048]{1,0:T(8,128)}, bf16[224,512]{1,0:T(8,128)(2,1)}, bf16[224,512]{1,0:T(8,128)(2,1)}, bf16[224,512]{1,0:T(8,128)(2,1)}, bf16[224,512]{1,0:T(8,128)(2,1)}) custom-call(bf16[2,512,224]{2,1,0:T(8,128)(2,1)S(1)} %get-tuple-element.16.hidt, bf16[2,16,224,128]{3,2,1,0:T(8,128)(2,1)S(1)} %get-tuple-element.17.gath, ...), custom_call_target="tpu_custom_call" | custom-call | tf_op jit(solution)/shard_map/weight_sums/pallas_call | solution.py:516
